TPU v7x, 256 devices: a whole 4x4x8 slice. The times are simulated.
256 devices in a mesh: blk: 64 (over y, z, core), band: 4 (over x).
Axes of the slice: x: 4, y: 4, z: 8, core: 2. Of those that a mesh axis runs over, the one named last changes fastest.
Arguments:
- sky_map: float32 [2, 512, 16384], P(None, 'blk'), may hold values from -6 to 6
- cycle_counts: int32 [512], P('blk'), may hold values from 8192 to 16384, as said below
- legendre: bfloat16 [512, 256, 4096], P(None, ('blk', 'band')), may hold values from -0.25 to 0.25
- signal_power: float32 [8192], replicated, may hold values from 0.1 to 10
- noise_power: float32 [8192], replicated, may hold values from 0.1 to 10
Outputs:
- filtered_map: float32 [2, 512, 16384], P(None, 'blk', 'band')
Inputs may be any that keep to these rules, and one draw needn't show every extreme that they name: `cycle_counts`: every cycle pair has between 8192 and 16384 pixels, and some cycle pair has exactly 16384.
All inputs are finite; a program needn't handle non-finite values.
Results may differ from a plain program's by a relative error of at most 0.0061.
Values may be sent and summed in bfloat16 or wider, within the bound.
A program may use at most 128 MiB of HBM per device.

v0:
```python
import math

import jax
import jax.numpy as jnp
from jax import lax
from jax.experimental import pallas as pl
from jax.experimental.pallas import tpu as pltpu
from jax.sharding import PartitionSpec as P

M_FIRST = 2048
N_BLK = 64
N_BAND = 4
R = 8
B = 128
A = 128
A_OWN = A // N_BAND
NR = N_BLK * R
NT = 4096
F32, BF16 = jnp.float32, jnp.bfloat16
MESH = pl.DeviceIdType.MESH
ROUND = 12582912.0
COEFS = (4.442882834158576, -7.308241154915532, 3.606288962930247, -0.8457636193361991, 0.10920579263730913)
DIMS_NT = (((1,), (1,)), ((), ()))


def cos_turns(x, period, inverse):
    whole = (x * inverse + ROUND) - ROUND
    t = (x - whole * period) * inverse
    u = t * t
    p = jnp.full_like(u, COEFS[-1])
    for c in COEFS[-2::-1]:
        p = p * u + c
    s = p * t
    return 1.0 - s * s


def iota(shape, dim):
    return lax.broadcasted_iota(jnp.int32, shape, dim)


def split(x):
    hi = x.astype(BF16)
    return hi, (x - hi.astype(F32)).astype(BF16)


def pixel_table(freq, count, inv_count):
    shape = (B // 8, 8, 128)
    odd = (2 * (iota(shape, 0) * 8 + iota(shape, 1)) + 1).astype(F32)
    quarter = jnp.where(iota((8, 128), 1) >= 64, 0.5 * count, 0.0)
    return cos_turns(odd * freq - quarter, 2.0 * count, 0.5 * inv_count)


def row_parts(first_row, rows, count, inv_count):
    shape = (rows // 8, 8, 128)
    slot = ((iota(shape, 0) * 8 + iota(shape, 1) + first_row) * B).astype(F32)
    near = jnp.where(slot > 0.5 * count, slot - count, slot)
    near = jnp.where(near > 0.5 * count, near - count, near)
    far = near * 1024.0
    far = far - ((far * inv_count + ROUND) - ROUND) * count
    return near, 2.0 * far


def row_table(parts, offset, count, inv_count):
    near, far = parts
    quarter = jnp.where(iota((8, 128), 1) >= 64, 0.25 * count, 0.0)
    return cos_turns(near * offset + (far - quarter), count, inv_count)


def kernel(
    counts, sky, leg, signal, noise, out,
    xs, legv, folded, send1, recv1, send2, recv2, modes, thi, tlo, wtab, wswap, gain, select,
    sky_sem, leg_sem, s1, r1, s2, r2, s3, r3,
):
    blk = lax.axis_index("blk")
    band = lax.axis_index("band")
    sky_copy = pltpu.make_async_copy(sky, xs, sky_sem)
    sky_copy.start()
    leg_copy = pltpu.make_async_copy(leg, legv, leg_sem)
    leg_copy.start()

    barrier = pltpu.get_barrier_semaphore()

    def greet(d, carry):
        pl.semaphore_signal(barrier, inc=1, device_id=(lax.rem(blk + d, N_BLK), band), device_id_type=MESH)
        return carry

    lax.fori_loop(1, N_BLK, greet, 0)
    for e in range(1, N_BAND):
        pl.semaphore_signal(barrier, inc=1, device_id=(blk, lax.rem(band + e, N_BAND)), device_id_type=MESH)

    lane = iota((8, 128), 1)
    own_offset = (lax.rem(lane, 64) * N_BAND + band).astype(F32)
    folded[...] = jnp.zeros_like(folded)
    sky_copy.wait()

    def count_of(r):
        count = jnp.full((8, 128), counts[r], jnp.int32).astype(F32)
        return count, 1.0 / count

    def analyse(r, carry):
        count, inv_count = count_of(r)
        table = pixel_table(own_offset + M_FIRST, count, inv_count).reshape(B, 128)
        t_hi, t_lo = split(table)
        turn = row_table(row_parts(0, A, count, inv_count), own_offset, count, inv_count)
        swapped = pltpu.roll(turn.reshape(A, 128), 64, 1).reshape(A // 8, 8, 128)
        pixels = xs[pl.ds(r, 2 * A, stride=R), :].reshape(2, A // 8, 8, 128)
        shape = (A // 8, 8, 128)
        slot = ((iota(shape, 0) * 8 + iota(shape, 1)) * B + iota(shape, 2)).astype(F32)
        pixels = jnp.where((slot < count)[None], pixels, 0.0).reshape(2 * A, B)
        x_hi, x_lo = split(pixels)
        part = jnp.dot(
            jnp.concatenate([x_hi, x_lo], axis=1), jnp.concatenate([t_hi, t_hi], axis=0), preferred_element_type=F32
        ) + jnp.dot(x_hi, t_lo, preferred_element_type=F32)
        part = part.reshape(2, A // 8, 8, 128)
        first = jnp.sum(part * turn[None], axis=1)
        second = jnp.sum(part * swapped[None], axis=1)
        first = jnp.concatenate([first[0], first[1]], axis=0)
        second = jnp.concatenate([second[0], second[1]], axis=0)
        scale = lax.rsqrt(count)
        scale = scale * (1.5 - 0.5 * count * scale * scale)
        scale2 = jnp.concatenate([scale, scale], axis=0)
        real = (first - pltpu.roll(first, 64, 1)) * scale2
        imag = -(second + pltpu.roll(second, 64, 1)) * scale2
        parts = (
            real[:8] + real[8:],
            imag[:8] + imag[8:],
            real[:8] - real[8:],
            imag[:8] - imag[8:],
        )
        for k, value in enumerate(parts):
            folded[pl.ds(r * 4 + k, 1), :] = jnp.sum(value, axis=0, keepdims=True)
        return carry

    lax.fori_loop(0, R, analyse, 0)

    turned = jnp.transpose(folded[...])[:N_BLK]
    turned_hi = turned.astype(BF16).astype(F32)
    turned_lo = turned - turned_hi
    lanes64 = iota((N_BLK, 128), 1)
    both = jnp.where(lanes64 < 32, turned_hi, jnp.where(lanes64 < 64, pltpu.roll(turned_lo, 32, 1), 0.0))
    send1[...] = both.reshape(N_BLK, 1, 128)

    pl.semaphore_wait(barrier, N_BLK - 1 + N_BAND - 1)

    def exchange(source, target, send_sem, recv_sem):
        def send(d, carry):
            peer = lax.rem(blk + d, N_BLK)
            pltpu.make_async_remote_copy(
                src_ref=source.at[peer],
                dst_ref=target.at[blk],
                send_sem=send_sem,
                recv_sem=recv_sem,
                device_id=(peer, band),
                device_id_type=MESH,
            ).start()
            return carry

        lax.fori_loop(1, N_BLK, send, 0)
        target[blk] = source[blk]
        return pltpu.make_async_remote_copy(
            src_ref=source.at[pl.ds(0, N_BLK - 1)],
            dst_ref=target.at[pl.ds(0, N_BLK - 1)],
            send_sem=send_sem,
            recv_sem=recv_sem,
            device_id=(blk, band),
            device_id_type=MESH,
        )

    done1 = exchange(send1, recv1, s1, r1)

    def prepare(r, carry):
        count, inv_count = count_of(r)
        parts = row_parts(band * A_OWN, A_OWN, count, inv_count)
        for c in range(N_BAND):
            offset = (lax.rem(lane, 64) * N_BAND + c).astype(F32)
            cols = pl.ds(c * 128, 128)
            hi, lo = split(pixel_table(offset + M_FIRST, count, inv_count).reshape(B, 128))
            thi[r, :, cols] = hi
            tlo[r, :, cols] = lo
            turn = row_table(parts, offset, count, inv_count).reshape(A_OWN, 128)
            wtab[r, :, cols] = turn
            wswap[r, :, cols] = pltpu.roll(turn, 64, 1)
        return carry

    lax.fori_loop(0, R, prepare, 0)

    order = blk * N_BAND + band
    low = lax.rem(order, 128)
    power = signal[...]
    rolled = pltpu.roll(power / (power + noise[...]), lax.rem(128 - low, 128), 1)
    gain[...] = rolled
    following = jnp.concatenate([gain[1:, :], gain[:1, :]], axis=0)
    gain[...] = jnp.where(lanes64 < 128 - low, rolled, following)
    first_gain = M_FIRST // 128 + order // 128

    shape = (512, 128)
    for k in range(4):
        select[k * NR : (k + 1) * NR, :] = jnp.where(
            iota(shape, 1) == lax.rem(iota(shape, 0), R) * 4 + k, 1.0, 0.0
        ).astype(BF16)
    comp = iota((8, 128), 0)
    lane_comp = jnp.where(comp < 4, lane, lane - 32)
    pick = jnp.where(
        (lane_comp >= 0) & (lane_comp < 32) & (lax.rem(lane_comp + 32, 4) == lax.rem(comp, 4)), 1.0, 0.0
    ).astype(BF16)

    leg_copy.wait()
    done1.wait_recv()

    shape = (N_BLK, 8, 128)
    here = (iota(shape, 2) < 64) & (lax.rem(iota(shape, 2), 32) // 4 == iota(shape, 1))
    spread = jnp.where(here, jnp.broadcast_to(recv1[...], shape), 0.0).reshape(NR, 128).astype(BF16)
    coeffs = lax.dot_general(pick, spread, DIMS_NT, preferred_element_type=F32).astype(BF16)
    sums = jnp.dot(coeffs, legv[...], preferred_element_type=F32)
    sums = sums + pltpu.roll(sums, 4, 0)
    other = pltpu.roll(sums, 2, 0)
    even = lax.rem(lane, 2) == 0
    upper = lax.rem(comp, 4) >= 2
    sign = jnp.where(upper & ~even, -1.0, 1.0)
    pieces = []
    for k in range(NT // 128):
        cols = slice(k * 128, (k + 1) * 128)
        row = gain[pl.ds(first_gain + k, 1), :]
        value = jnp.where(even ^ upper, sums[:, cols], other[:, cols]) * (row * sign)
        hi = value.astype(BF16).astype(F32)
        pieces.append(jnp.where(comp < 4, hi, value - hi).astype(BF16))
    filtered = jnp.concatenate(pieces, axis=1)
    cycle = lax.dot_general(filtered, legv[...], DIMS_NT, preferred_element_type=F32)
    cycle = cycle + pltpu.roll(cycle, 4, 0)
    shape = (N_BLK, NR)
    own_block = iota(shape, 1) // R == iota(shape, 0)
    blocks = [
        jnp.where(own_block, jnp.broadcast_to(cycle[k : k + 1, :], shape), 0.0).astype(BF16) for k in range(4)
    ]
    rows = jnp.dot(jnp.concatenate(blocks, axis=1), select[...], preferred_element_type=F32)
    send2[...] = rows.reshape(N_BLK, 1, 128)
    done2 = exchange(send2, recv2, s2, r2)
    done2.wait_recv()

    got = recv2[...].reshape(N_BLK, 128)
    got = jnp.transpose(jnp.concatenate([got, got], axis=0))[:32]
    shape = (32, 128)
    is_imag = lax.rem(iota(shape, 0), 2) == 1
    norm = 1.0 / math.sqrt(N_BLK * N_BAND)
    modes[band] = got * jnp.where(is_imag | (iota(shape, 1) >= 64), -norm, norm)
    for e in range(1, N_BAND):
        pltpu.make_async_remote_copy(
            src_ref=modes.at[band],
            dst_ref=modes.at[band],
            send_sem=s3,
            recv_sem=r3,
            device_id=(blk, lax.rem(band + e, N_BAND)),
            device_id_type=MESH,
        ).start()
    done3 = pltpu.make_async_remote_copy(
        src_ref=modes.at[pl.ds(0, N_BAND - 1)],
        dst_ref=modes.at[pl.ds(0, N_BAND - 1)],
        send_sem=s3,
        recv_sem=r3,
        device_id=(blk, band),
        device_id_type=MESH,
    )
    done3.wait_recv()

    def synthesise(r, carry):
        halves = []
        for h in range(2):
            cols = []
            for c in range(N_BAND):
                re = modes[c, pl.ds(r * 4 + 2 * h, 1), :]
                im = modes[c, pl.ds(r * 4 + 2 * h + 1, 1), :]
                at = pl.ds(c * 128, 128)
                cols.append(wtab[r, :, at] * re + wswap[r, :, at] * im)
            halves.append(jnp.concatenate(cols, axis=1))
        z_hi, z_lo = split(jnp.concatenate(halves, axis=0))
        rows = 2 * A_OWN
        t_hi, t_lo = thi[r], tlo[r]
        main = lax.dot_general(jnp.concatenate([z_hi, z_lo], axis=0), t_hi, DIMS_NT, preferred_element_type=F32)
        value = main[:rows] + main[rows:] + lax.dot_general(z_hi, t_lo, DIMS_NT, preferred_element_type=F32)
        shape = (rows, B)
        slot = (lax.rem(iota(shape, 0), A_OWN) + band * A_OWN) * B + iota(shape, 1)
        out[pl.ds(r, rows, stride=R), :] = jnp.where(slot < counts[r], value, 0.0)
        return carry

    lax.fori_loop(0, R, synthesise, 0)
    done1.wait_send()
    done2.wait_send()
    done3.wait_send()


def per_device(sky_map, cycle_counts, legendre, signal_power, noise_power):
    sky = sky_map.reshape(2, R, A, B).transpose(0, 2, 1, 3).reshape(2 * A * R, B)
    leg = legendre.reshape(NR, NT)
    vmem = pl.BlockSpec(memory_space=pltpu.VMEM)
    anywhere = pl.BlockSpec(memory_space=pl.ANY)
    dma = pltpu.SemaphoreType.DMA
    result = pl.pallas_call(
        kernel,
        out_shape=jax.ShapeDtypeStruct((2 * A_OWN * R, B), F32),
        in_specs=[pl.BlockSpec(memory_space=pltpu.SMEM), anywhere, anywhere, vmem, vmem],
        out_specs=vmem,
        scratch_shapes=[
            pltpu.VMEM((2 * A * R, B), F32),
            pltpu.VMEM((NR, NT), BF16),
            pltpu.VMEM((128, 128), F32),
            pltpu.VMEM((N_BLK, 1, 128), F32),
            pltpu.VMEM((N_BLK, 1, 128), F32),
            pltpu.VMEM((N_BLK, 1, 128), F32),
            pltpu.VMEM((N_BLK, 1, 128), F32),
            pltpu.VMEM((N_BAND, 32, 128), F32),
            pltpu.VMEM((R, B, N_BAND * 128), BF16),
            pltpu.VMEM((R, B, N_BAND * 128), BF16),
            pltpu.VMEM((R, A_OWN, N_BAND * 128), F32),
            pltpu.VMEM((R, A_OWN, N_BAND * 128), F32),
            pltpu.VMEM((64, 128), F32),
            pltpu.VMEM((4 * NR, 128), BF16),
            dma, dma, dma, dma, dma, dma, dma, dma,
        ],
        compiler_params=pltpu.CompilerParams(collective_id=0, has_side_effects=True, vmem_limit_bytes=67043328),
    )(cycle_counts, sky, leg, signal_power.reshape(64, 128), noise_power.reshape(64, 128))
    return result.reshape(2, A_OWN, R, B).transpose(0, 2, 1, 3).reshape(2, R, A_OWN * B)


def solution(mesh):
    placed = (P(None, "blk", None), P("blk"), P(None, ("blk", "band"), None), P(), P())
    return jax.shard_map(
        per_device, mesh=mesh, in_specs=placed, out_specs=P(None, "blk", "band"), check_vma=False
    )
```

profile of v0, /device:TPU:1, one launch (start us, length us, event | category | flops | bytes accessed | tf_op | source)
XLA Modules:
  0.0 34.2 jit_solution(3721863714438465586)
XLA Ops:
  0.0 32.6 %shard_map.55 = f32[512,128]{1,0:T(8,128)} custom-call(s32[8]{0:T(128)} %counts.1, f32[2048,128]{1,0:T(8,128)} %bitcast.15, bf16[512,4096]{1,0:T(8,128)(2,1)} %bitcast.13, f32[64,128]{1,0:T(8,128)} %bitcast.16, f32[64,128]{1,0:T(8,128)} %bitcast.17), custom_call_target="tpu_custom_call" | custom-call | tf_op jit(solution)/shard_map/pallas_call | solution.py:297
  32.6 1.7 %copy.7 = f32[2,8,4096]{2,1,0:T(8,128)} copy(f32[2,8,4096]{2,1,0:T(8,128)} %bitcast.14) | data formatting | bytes 524288
where the time goes:
time: 34.4 us; the launch traced here: 34.2 us
  Pallas kernels  32.6 us (95%)
  local copies, waits for them, and re-layouts  1.67 us (5%)
    pallas_call x1, Pallas kernels, per_device(): pl.pallas_call(kernel, out_shape=jax.ShapeDtypeStruct((2 * A_OWN * R, B),...  32.6 us
    unnamed x1, local copies, waits for them, and re-layouts  1.67 us

commit v1 on v0

--- a/solution.py
+++ b/solution.py
@@ -67,30 +67,40 @@
 
 
 def kernel(
-    counts, sky, leg, signal, noise, out,
-    xs, legv, folded, send1, recv1, send2, recv2, modes, thi, tlo, wtab, wswap, gain, select,
-    sky_sem, leg_sem, s1, r1, s2, r2, s3, r3,
+    counts_in, sky, leg, signal_in, noise_in, out,
+    counts, xs, legv, signal, noise, folded, send1, recv1, send2, recv2, modes, along, across, table, wtab, wswap, gain, select,
+    count_sem, sky_sem, leg_sem, signal_sem, noise_sem, s1, r1, s2, r2, s3, r3,
 ):
     blk = lax.axis_index("blk")
     band = lax.axis_index("band")
+    barrier = pltpu.get_barrier_semaphore()
+
+    ys = [lax.rem(lax.div(blk, 16) + d, 4) * 16 for d in range(4)]
+    zs = [lax.rem(lax.rem(lax.div(blk, 2), 8) + d, 8) * 2 for d in range(8)]
+    cs = [lax.rem(blk + d, 2) for d in range(2)]
+    steps = [(y, z, c) for y in range(4) for z in range(8) for c in range(2)][1:]
+    steps.sort(key=lambda s: -min(s[0], 4 - s[0]) - min(s[1], 8 - s[1]))
+    peers = [ys[y] + zs[z] + cs[c] for y, z, c in steps]
+
+    for peer in peers:
+        pl.semaphore_signal(barrier, inc=1, device_id=(peer, band), device_id_type=MESH)
+    for e in range(1, N_BAND):
+        pl.semaphore_signal(barrier, inc=1, device_id=(blk, lax.rem(band + e, N_BAND)), device_id_type=MESH)
+    count_copy = pltpu.make_async_copy(counts_in, counts, count_sem)
+    count_copy.start()
     sky_copy = pltpu.make_async_copy(sky, xs, sky_sem)
     sky_copy.start()
     leg_copy = pltpu.make_async_copy(leg, legv, leg_sem)
     leg_copy.start()
-
-    barrier = pltpu.get_barrier_semaphore()
-
-    def greet(d, carry):
-        pl.semaphore_signal(barrier, inc=1, device_id=(lax.rem(blk + d, N_BLK), band), device_id_type=MESH)
-        return carry
-
-    lax.fori_loop(1, N_BLK, greet, 0)
-    for e in range(1, N_BAND):
-        pl.semaphore_signal(barrier, inc=1, device_id=(blk, lax.rem(band + e, N_BAND)), device_id_type=MESH)
+    signal_copy = pltpu.make_async_copy(signal_in, signal, signal_sem)
+    signal_copy.start()
+    noise_copy = pltpu.make_async_copy(noise_in, noise, noise_sem)
+    noise_copy.start()
 
     lane = iota((8, 128), 1)
     own_offset = (lax.rem(lane, 64) * N_BAND + band).astype(F32)
     folded[...] = jnp.zeros_like(folded)
+    count_copy.wait()
     sky_copy.wait()
 
     def count_of(r):
@@ -143,8 +153,7 @@
     pl.semaphore_wait(barrier, N_BLK - 1 + N_BAND - 1)
 
     def exchange(source, target, send_sem, recv_sem):
-        def send(d, carry):
-            peer = lax.rem(blk + d, N_BLK)
+        for peer in peers:
             pltpu.make_async_remote_copy(
                 src_ref=source.at[peer],
                 dst_ref=target.at[blk],
@@ -153,9 +162,6 @@
                 device_id=(peer, band),
                 device_id_type=MESH,
             ).start()
-            return carry
-
-        lax.fori_loop(1, N_BLK, send, 0)
         target[blk] = source[blk]
         return pltpu.make_async_remote_copy(
             src_ref=source.at[pl.ds(0, N_BLK - 1)],
@@ -174,9 +180,7 @@
         for c in range(N_BAND):
             offset = (lax.rem(lane, 64) * N_BAND + c).astype(F32)
             cols = pl.ds(c * 128, 128)
-            hi, lo = split(pixel_table(offset + M_FIRST, count, inv_count).reshape(B, 128))
-            thi[r, :, cols] = hi
-            tlo[r, :, cols] = lo
+            table[r, :, cols] = pixel_table(offset + M_FIRST, count, inv_count).reshape(B, 128).astype(BF16)
             turn = row_table(parts, offset, count, inv_count).reshape(A_OWN, 128)
             wtab[r, :, cols] = turn
             wswap[r, :, cols] = pltpu.roll(turn, 64, 1)
@@ -186,6 +190,8 @@
 
     order = blk * N_BAND + band
     low = lax.rem(order, 128)
+    signal_copy.wait()
+    noise_copy.wait()
     power = signal[...]
     rolled = pltpu.roll(power / (power + noise[...]), lax.rem(128 - low, 128), 1)
     gain[...] = rolled
@@ -237,12 +243,10 @@
     done2 = exchange(send2, recv2, s2, r2)
     done2.wait_recv()
 
-    got = recv2[...].reshape(N_BLK, 128)
-    got = jnp.transpose(jnp.concatenate([got, got], axis=0))[:32]
-    shape = (32, 128)
-    is_imag = lax.rem(iota(shape, 0), 2) == 1
-    norm = 1.0 / math.sqrt(N_BLK * N_BAND)
-    modes[band] = got * jnp.where(is_imag | (iota(shape, 1) >= 64), -norm, norm)
+    got = jnp.transpose(jnp.concatenate([recv2[...].reshape(N_BLK, 128)] * 2, axis=0))[:32]
+    got = got.reshape(16, 2, 128)
+    shape = (16, 128)
+    modes[band] = jnp.where(iota(shape, 1) < 64, got[:, 0], got[:, 1]).astype(BF16)
     for e in range(1, N_BAND):
         pltpu.make_async_remote_copy(
             src_ref=modes.at[band],
@@ -262,24 +266,28 @@
     )
     done3.wait_recv()
 
+    shape = (N_BAND, 16, 128)
+    norm = 1.0 / math.sqrt(N_BLK * N_BAND)
+    got = modes[...].astype(F32) * norm
+    turned = pltpu.roll(got, 64, 2)
+    left = iota(shape, 2) < 64
+    along[...] = jnp.where(left, got, -turned)
+    across[...] = jnp.where(left, -turned, -got)
+
     def synthesise(r, carry):
         halves = []
         for h in range(2):
             cols = []
             for c in range(N_BAND):
-                re = modes[c, pl.ds(r * 4 + 2 * h, 1), :]
-                im = modes[c, pl.ds(r * 4 + 2 * h + 1, 1), :]
+                row = pl.ds(r * 2 + h, 1)
                 at = pl.ds(c * 128, 128)
-                cols.append(wtab[r, :, at] * re + wswap[r, :, at] * im)
+                cols.append(wtab[r, :, at] * along[c, row, :] + wswap[r, :, at] * across[c, row, :])
             halves.append(jnp.concatenate(cols, axis=1))
-        z_hi, z_lo = split(jnp.concatenate(halves, axis=0))
-        rows = 2 * A_OWN
-        t_hi, t_lo = thi[r], tlo[r]
-        main = lax.dot_general(jnp.concatenate([z_hi, z_lo], axis=0), t_hi, DIMS_NT, preferred_element_type=F32)
-        value = main[:rows] + main[rows:] + lax.dot_general(z_hi, t_lo, DIMS_NT, preferred_element_type=F32)
-        shape = (rows, B)
+        z = jnp.concatenate(halves, axis=0).astype(BF16)
+        value = lax.dot_general(z, table[r], DIMS_NT, preferred_element_type=F32)
+        shape = (2 * A_OWN, B)
         slot = (lax.rem(iota(shape, 0), A_OWN) + band * A_OWN) * B + iota(shape, 1)
-        out[pl.ds(r, rows, stride=R), :] = jnp.where(slot < counts[r], value, 0.0)
+        out[pl.ds(r, 2 * A_OWN, stride=R), :] = jnp.where(slot < counts[r], value, 0.0)
         return carry
 
     lax.fori_loop(0, R, synthesise, 0)
@@ -297,24 +305,28 @@
     result = pl.pallas_call(
         kernel,
         out_shape=jax.ShapeDtypeStruct((2 * A_OWN * R, B), F32),
-        in_specs=[pl.BlockSpec(memory_space=pltpu.SMEM), anywhere, anywhere, vmem, vmem],
+        in_specs=[anywhere] * 5,
         out_specs=vmem,
         scratch_shapes=[
+            pltpu.SMEM((R,), jnp.int32),
             pltpu.VMEM((2 * A * R, B), F32),
             pltpu.VMEM((NR, NT), BF16),
+            pltpu.VMEM((64, 128), F32),
+            pltpu.VMEM((64, 128), F32),
             pltpu.VMEM((128, 128), F32),
             pltpu.VMEM((N_BLK, 1, 128), F32),
             pltpu.VMEM((N_BLK, 1, 128), F32),
             pltpu.VMEM((N_BLK, 1, 128), F32),
             pltpu.VMEM((N_BLK, 1, 128), F32),
-            pltpu.VMEM((N_BAND, 32, 128), F32),
-            pltpu.VMEM((R, B, N_BAND * 128), BF16),
+            pltpu.VMEM((N_BAND, 16, 128), BF16),
+            pltpu.VMEM((N_BAND, 16, 128), F32),
+            pltpu.VMEM((N_BAND, 16, 128), F32),
             pltpu.VMEM((R, B, N_BAND * 128), BF16),
             pltpu.VMEM((R, A_OWN, N_BAND * 128), F32),
             pltpu.VMEM((R, A_OWN, N_BAND * 128), F32),
             pltpu.VMEM((64, 128), F32),
             pltpu.VMEM((4 * NR, 128), BF16),
-            dma, dma, dma, dma, dma, dma, dma, dma,
+            *([dma] * 11),
         ],
         compiler_params=pltpu.CompilerParams(collective_id=0, has_side_effects=True, vmem_limit_bytes=67043328),
     )(cycle_counts, sky, leg, signal_power.reshape(64, 128), noise_power.reshape(64, 128))

time: 34.4 us -> 32 us (0.930)
  Pallas kernels: 32.6 us -> 30.2 us
    pallas_call x1, Pallas kernels: 32.6 us -> 30.2 us  [per_device(): pl.pallas_call(kernel, out_shape=jax.ShapeDtypeStruct((2 * A_OWN * R, B),...]
where the time goes in v1:
time: 32 us; the launch traced here: 31.9 us
  Pallas kernels  30.2 us (94%)
  local copies, waits for them, and re-layouts  1.67 us (5%)
    pallas_call x1, Pallas kernels, per_device(): pl.pallas_call(kernel, out_shape=jax.ShapeDtypeStruct((2 * A_OWN * R, B),...  30.2 us
    unnamed x1, local copies, waits for them, and re-layouts  1.67 us

profile of v1, /device:TPU:1, one launch (start us, length us, event | category | flops | bytes accessed | tf_op | source)
XLA Modules:
  0.0 31.9 jit_solution(4830603787611397574)
XLA Ops:
  0.0 30.2 %shard_map.55 = f32[512,128]{1,0:T(8,128)} custom-call(s32[8]{0:T(128)} %counts_in.1, f32[2048,128]{1,0:T(8,128)} %bitcast.15, bf16[512,4096]{1,0:T(8,128)(2,1)} %bitcast.13, f32[64,128]{1,0:T(8,128)} %bitcast.16, f32[64,128]{1,0:T(8,128)} %bitcast.17), custom_call_target="tpu_custom_call" | custom-call | tf_op jit(solution)/shard_map/pallas_call | solution.py:305
  30.2 1.7 %copy.7 = f32[2,8,4096]{2,1,0:T(8,128)} copy(f32[2,8,4096]{2,1,0:T(8,128)} %bitcast.14) | data formatting | bytes 524288

commit v2 on v1

--- a/solution.py
+++ b/solution.py
@@ -50,6 +50,15 @@
     return cos_turns(odd * freq - quarter, 2.0 * count, 0.5 * inv_count)
 
 
+def order_table(c, sines, count, inv_count):
+    shape = (8, 8, 128)
+    row = iota(shape, 0) * 8 + iota(shape, 1)
+    freq = (row * N_BAND + (M_FIRST + c)).astype(F32)
+    odd = (2 * iota((8, 128), 1) + 1).astype(F32)
+    x = freq * odd
+    return cos_turns(x + 0.5 * count if sines else x, 2.0 * count, 0.5 * inv_count)
+
+
 def row_parts(first_row, rows, count, inv_count):
     shape = (rows // 8, 8, 128)
     slot = ((iota(shape, 0) * 8 + iota(shape, 1) + first_row) * B).astype(F32)
@@ -60,16 +69,15 @@
     return near, 2.0 * far
 
 
-def row_table(parts, offset, count, inv_count):
+def row_table(parts, offset, count, inv_count, quarter):
     near, far = parts
-    quarter = jnp.where(iota((8, 128), 1) >= 64, 0.25 * count, 0.0)
     return cos_turns(near * offset + (far - quarter), count, inv_count)
 
 
 def kernel(
     counts_in, sky, leg, signal_in, noise_in, out,
-    counts, xs, legv, signal, noise, folded, send1, recv1, send2, recv2, modes, along, across, table, wtab, wswap, gain, select,
-    count_sem, sky_sem, leg_sem, signal_sem, noise_sem, s1, r1, s2, r2, s3, r3,
+    counts, xs, legv, signal, noise, folded, send1, recv1, send2, recv2, modes, table, wcos, wsin, gain, select,
+    count_sem, sky_sem, leg_sem, signal_sem, noise_sem, s1, r1, s2, r2,
 ):
     blk = lax.axis_index("blk")
     band = lax.axis_index("band")
@@ -80,6 +88,10 @@
     cs = [lax.rem(blk + d, 2) for d in range(2)]
     steps = [(y, z, c) for y in range(4) for z in range(8) for c in range(2)][1:]
     steps.sort(key=lambda s: -min(s[0], 4 - s[0]) - min(s[1], 8 - s[1]))
+    everyone = [(x, s) for x in range(N_BAND) for s in [(0, 0, 0)] + steps][1:]
+    everyone.sort(key=lambda t: -min(t[0], 4 - t[0]) - min(t[1][0], 4 - t[1][0]) - min(t[1][1], 8 - t[1][1]))
+    bands = [lax.rem(band + x, N_BAND) for x in range(N_BAND)]
+    everyone = [(ys[y] + zs[z] + cs[c], bands[x]) for x, (y, z, c) in everyone]
     peers = [ys[y] + zs[z] + cs[c] for y, z, c in steps]
 
     for peer in peers:
@@ -111,7 +123,8 @@
         count, inv_count = count_of(r)
         table = pixel_table(own_offset + M_FIRST, count, inv_count).reshape(B, 128)
         t_hi, t_lo = split(table)
-        turn = row_table(row_parts(0, A, count, inv_count), own_offset, count, inv_count)
+        quarter = jnp.where(lane >= 64, 0.25 * count, 0.0)
+        turn = row_table(row_parts(0, A, count, inv_count), own_offset, count, inv_count, quarter)
         swapped = pltpu.roll(turn.reshape(A, 128), 64, 1).reshape(A // 8, 8, 128)
         pixels = xs[pl.ds(r, 2 * A, stride=R), :].reshape(2, A // 8, 8, 128)
         shape = (A // 8, 8, 128)
@@ -178,12 +191,13 @@
         count, inv_count = count_of(r)
         parts = row_parts(band * A_OWN, A_OWN, count, inv_count)
         for c in range(N_BAND):
-            offset = (lax.rem(lane, 64) * N_BAND + c).astype(F32)
-            cols = pl.ds(c * 128, 128)
-            table[r, :, cols] = pixel_table(offset + M_FIRST, count, inv_count).reshape(B, 128).astype(BF16)
-            turn = row_table(parts, offset, count, inv_count).reshape(A_OWN, 128)
-            wtab[r, :, cols] = turn
-            wswap[r, :, cols] = pltpu.roll(turn, 64, 1)
+            table[r, pl.ds(c * 64, 64), :] = order_table(c, False, count, inv_count).reshape(64, B).astype(BF16)
+            table[r, pl.ds(256 + c * 64, 64), :] = order_table(c, True, count, inv_count).reshape(64, B).astype(BF16)
+        for p in range(2):
+            offset = (lax.rem(lane, 64) * N_BAND + lax.div(lane, 64) + 2 * p).astype(F32)
+            cols = pl.ds(p * 128, 128)
+            wcos[r, :, cols] = row_table(parts, offset, count, inv_count, 0.0).reshape(A_OWN, 128)
+            wsin[r, :, cols] = row_table(parts, offset, count, inv_count, 0.25 * count).reshape(A_OWN, 128)
         return carry
 
     lax.fori_loop(0, R, prepare, 0)
@@ -240,67 +254,55 @@
     ]
     rows = jnp.dot(jnp.concatenate(blocks, axis=1), select[...], preferred_element_type=F32)
     send2[...] = rows.reshape(N_BLK, 1, 128)
-    done2 = exchange(send2, recv2, s2, r2)
-    done2.wait_recv()
-
-    got = jnp.transpose(jnp.concatenate([recv2[...].reshape(N_BLK, 128)] * 2, axis=0))[:32]
-    got = got.reshape(16, 2, 128)
-    shape = (16, 128)
-    modes[band] = jnp.where(iota(shape, 1) < 64, got[:, 0], got[:, 1]).astype(BF16)
-    for e in range(1, N_BAND):
+    for peer, to in everyone:
         pltpu.make_async_remote_copy(
-            src_ref=modes.at[band],
-            dst_ref=modes.at[band],
-            send_sem=s3,
-            recv_sem=r3,
-            device_id=(blk, lax.rem(band + e, N_BAND)),
+            src_ref=send2.at[peer],
+            dst_ref=recv2.at[band * N_BLK + blk],
+            send_sem=s2,
+            recv_sem=r2,
+            device_id=(peer, to),
             device_id_type=MESH,
         ).start()
-    done3 = pltpu.make_async_remote_copy(
-        src_ref=modes.at[pl.ds(0, N_BAND - 1)],
-        dst_ref=modes.at[pl.ds(0, N_BAND - 1)],
-        send_sem=s3,
-        recv_sem=r3,
+    recv2[band * N_BLK + blk] = send2[blk]
+    done2 = pltpu.make_async_remote_copy(
+        src_ref=recv2.at[pl.ds(0, N_BLK * N_BAND - 1)],
+        dst_ref=recv2.at[pl.ds(0, N_BLK * N_BAND - 1)],
+        send_sem=s2,
+        recv_sem=r2,
         device_id=(blk, band),
         device_id_type=MESH,
     )
-    done3.wait_recv()
-
-    shape = (N_BAND, 16, 128)
+    done2.wait_recv()
+
     norm = 1.0 / math.sqrt(N_BLK * N_BAND)
-    got = modes[...].astype(F32) * norm
-    turned = pltpu.roll(got, 64, 2)
-    left = iota(shape, 2) < 64
-    along[...] = jnp.where(left, got, -turned)
-    across[...] = jnp.where(left, -turned, -got)
+    for p in range(2):
+        got = jnp.transpose(recv2[pl.ds(p * 128, 128)].reshape(128, 128))[:32]
+        modes[:, p * 128 : (p + 1) * 128] = got * norm
 
     def synthesise(r, carry):
         halves = []
         for h in range(2):
-            cols = []
-            for c in range(N_BAND):
-                row = pl.ds(r * 2 + h, 1)
-                at = pl.ds(c * 128, 128)
-                cols.append(wtab[r, :, at] * along[c, row, :] + wswap[r, :, at] * across[c, row, :])
-            halves.append(jnp.concatenate(cols, axis=1))
+            re = modes[pl.ds(r * 4 + 2 * h, 1), :]
+            im = modes[pl.ds(r * 4 + 2 * h + 1, 1), :]
+            cosines, sines = wcos[r], wsin[r]
+            halves.append(jnp.concatenate([cosines * re - sines * im, sines * re + cosines * im], axis=1))
         z = jnp.concatenate(halves, axis=0).astype(BF16)
-        value = lax.dot_general(z, table[r], DIMS_NT, preferred_element_type=F32)
+        value = jnp.dot(z, table[r], preferred_element_type=F32)
         shape = (2 * A_OWN, B)
         slot = (lax.rem(iota(shape, 0), A_OWN) + band * A_OWN) * B + iota(shape, 1)
         out[pl.ds(r, 2 * A_OWN, stride=R), :] = jnp.where(slot < counts[r], value, 0.0)
         return carry
 
-    lax.fori_loop(0, R, synthesise, 0)
+    lax.fori_loop(0, R, synthesise, 0, unroll=True)
     done1.wait_send()
     done2.wait_send()
-    done3.wait_send()
 
 
 def per_device(sky_map, cycle_counts, legendre, signal_power, noise_power):
     sky = sky_map.reshape(2, R, A, B).transpose(0, 2, 1, 3).reshape(2 * A * R, B)
     leg = legendre.reshape(NR, NT)
     vmem = pl.BlockSpec(memory_space=pltpu.VMEM)
-    anywhere = pl.BlockSpec(memory_space=pl.ANY)
+    anywhere = pl.BlockSpec(memory_space=pltpu.HBM)
     dma = pltpu.SemaphoreType.DMA
     result = pl.pallas_call(
         kernel,
@@ -317,16 +319,14 @@
             pltpu.VMEM((N_BLK, 1, 128), F32),
             pltpu.VMEM((N_BLK, 1, 128), F32),
             pltpu.VMEM((N_BLK, 1, 128), F32),
-            pltpu.VMEM((N_BLK, 1, 128), F32),
-            pltpu.VMEM((N_BAND, 16, 128), BF16),
-            pltpu.VMEM((N_BAND, 16, 128), F32),
-            pltpu.VMEM((N_BAND, 16, 128), F32),
-            pltpu.VMEM((R, B, N_BAND * 128), BF16),
-            pltpu.VMEM((R, A_OWN, N_BAND * 128), F32),
-            pltpu.VMEM((R, A_OWN, N_BAND * 128), F32),
+            pltpu.VMEM((N_BAND * N_BLK, 1, 128), F32),
+            pltpu.VMEM((32, N_BAND * 64), F32),
+            pltpu.VMEM((R, N_BAND * 128, B), BF16),
+            pltpu.VMEM((R, A_OWN, N_BAND * 64), F32),
+            pltpu.VMEM((R, A_OWN, N_BAND * 64), F32),
             pltpu.VMEM((64, 128), F32),
             pltpu.VMEM((4 * NR, 128), BF16),
-            *([dma] * 11),
+            *([dma] * 9),
         ],
         compiler_params=pltpu.CompilerParams(collective_id=0, has_side_effects=True, vmem_limit_bytes=67043328),
     )(cycle_counts, sky, leg, signal_power.reshape(64, 128), noise_power.reshape(64, 128))

time: 32 us -> 30.1 us (0.941)
  Pallas kernels: 30.2 us -> 28.3 us
    pallas_call x1, Pallas kernels: 30.2 us -> 28.3 us  [per_device(): pl.pallas_call(kernel, out_shape=jax.ShapeDtypeStruct((2 * A_OWN * R, B),...]
where the time goes in v2:
time: 30.1 us; the launch traced here: 30 us
  Pallas kernels  28.3 us (94%)
  local copies, waits for them, and re-layouts  1.67 us (6%)
    pallas_call x1, Pallas kernels, per_device(): pl.pallas_call(kernel, out_shape=jax.ShapeDtypeStruct((2 * A_OWN * R, B),...  28.3 us
    unnamed x1, local copies, waits for them, and re-layouts  1.67 us

profile of v2, /device:TPU:1, one launch (start us, length us, event | category | flops | bytes accessed | tf_op | source)
XLA Modules:
  0.0 30.0 jit_solution(644284174789629913)
XLA Ops:
  0.0 28.3 %shard_map.55 = f32[512,128]{1,0:T(8,128)} custom-call(s32[8]{0:T(128)} %counts_in.1, f32[2048,128]{1,0:T(8,128)} %bitcast.15, bf16[512,4096]{1,0:T(8,128)(2,1)} %bitcast.13, f32[64,128]{1,0:T(8,128)} %bitcast.16, f32[64,128]{1,0:T(8,128)} %bitcast.17), custom_call_target="tpu_custom_call" | custom-call | tf_op jit(solution)/shard_map/pallas_call | solution.py:307
  28.4 1.7 %copy.7 = f32[2,8,4096]{2,1,0:T(8,128)} copy(f32[2,8,4096]{2,1,0:T(8,128)} %bitcast.14) | data formatting | bytes 524288

commit v3 on v2

--- a/solution.py
+++ b/solution.py
@@ -76,7 +76,7 @@
 
 def kernel(
     counts_in, sky, leg, signal_in, noise_in, out,
-    counts, xs, legv, signal, noise, folded, send1, recv1, send2, recv2, modes, table, wcos, wsin, gain, select,
+    counts, xs, legv, leg_turned, signal, noise, folded, send1, recv1, send2, recv2, modes, table, wcos, wsin, gain, select,
     count_sem, sky_sem, leg_sem, signal_sem, noise_sem, s1, r1, s2, r2,
 ):
     blk = lax.axis_index("blk")
@@ -202,6 +202,15 @@
 
     lax.fori_loop(0, R, prepare, 0)
 
+    leg_copy.wait()
+
+    def turn_legendre(k, carry):
+        cols = pl.ds(pl.multiple_of(k * 128, 128), 128)
+        leg_turned[cols, :] = jnp.transpose(legv[:, cols])
+        return carry
+
+    lax.fori_loop(0, NT // 128, turn_legendre, 0, unroll=2)
+
     order = blk * N_BAND + band
     low = lax.rem(order, 128)
     signal_copy.wait()
@@ -213,18 +222,20 @@
     gain[...] = jnp.where(lanes64 < 128 - low, rolled, following)
     first_gain = M_FIRST // 128 + order // 128
 
-    shape = (512, 128)
-    for k in range(4):
-        select[k * NR : (k + 1) * NR, :] = jnp.where(
-            iota(shape, 1) == lax.rem(iota(shape, 0), R) * 4 + k, 1.0, 0.0
-        ).astype(BF16)
+    def permute(k, carry):
+        rows = pl.ds(pl.multiple_of(k * 64, 64), 64)
+        source = iota((64, NR), 0) + k * 64
+        column = iota((64, NR), 1)
+        select[rows, :] = jnp.where(lax.rem(column, N_BLK) * R + column // N_BLK == source, 1.0, 0.0).astype(BF16)
+        return carry
+
+    lax.fori_loop(0, NR // 64, permute, 0)
     comp = iota((8, 128), 0)
     lane_comp = jnp.where(comp < 4, lane, lane - 32)
     pick = jnp.where(
         (lane_comp >= 0) & (lane_comp < 32) & (lax.rem(lane_comp + 32, 4) == lax.rem(comp, 4)), 1.0, 0.0
     ).astype(BF16)
 
-    leg_copy.wait()
     done1.wait_recv()
 
     shape = (N_BLK, 8, 128)
@@ -245,14 +256,12 @@
         hi = value.astype(BF16).astype(F32)
         pieces.append(jnp.where(comp < 4, hi, value - hi).astype(BF16))
     filtered = jnp.concatenate(pieces, axis=1)
-    cycle = lax.dot_general(filtered, legv[...], DIMS_NT, preferred_element_type=F32)
+    cycle = jnp.dot(filtered, leg_turned[...], preferred_element_type=F32)
     cycle = cycle + pltpu.roll(cycle, 4, 0)
-    shape = (N_BLK, NR)
-    own_block = iota(shape, 1) // R == iota(shape, 0)
-    blocks = [
-        jnp.where(own_block, jnp.broadcast_to(cycle[k : k + 1, :], shape), 0.0).astype(BF16) for k in range(4)
-    ]
-    rows = jnp.dot(jnp.concatenate(blocks, axis=1), select[...], preferred_element_type=F32)
+    cycle = jnp.dot(cycle.astype(BF16), select[...], preferred_element_type=F32)
+    stack = jnp.concatenate([cycle[:, k * 128 : (k + 1) * 128] for k in range(4)], axis=0)
+    stack = jnp.transpose(jnp.concatenate([stack, jnp.zeros((96, 128), F32)], axis=0))
+    rows = stack[:N_BLK] + pltpu.roll(stack[N_BLK:], 32, 1)
     send2[...] = rows.reshape(N_BLK, 1, 128)
     for peer, to in everyone:
         pltpu.make_async_remote_copy(
@@ -276,14 +285,15 @@
 
     norm = 1.0 / math.sqrt(N_BLK * N_BAND)
     for p in range(2):
-        got = jnp.transpose(recv2[pl.ds(p * 128, 128)].reshape(128, 128))[:32]
+        got = jnp.transpose(recv2[pl.ds(p * 128, 128)].reshape(128, 128))[:64]
         modes[:, p * 128 : (p + 1) * 128] = got * norm
 
     def synthesise(r, carry):
         halves = []
         for h in range(2):
-            re = modes[pl.ds(r * 4 + 2 * h, 1), :]
-            im = modes[pl.ds(r * 4 + 2 * h + 1, 1), :]
+            at = lax.rem(r, 2) * 32 + r // 2 * 8 + 2 * h
+            re = modes[pl.ds(at, 1), :]
+            im = modes[pl.ds(at + 1, 1), :]
             cosines, sines = wcos[r], wsin[r]
             halves.append(jnp.concatenate([cosines * re - sines * im, sines * re + cosines * im], axis=1))
         z = jnp.concatenate(halves, axis=0).astype(BF16)
@@ -313,6 +323,7 @@
             pltpu.SMEM((R,), jnp.int32),
             pltpu.VMEM((2 * A * R, B), F32),
             pltpu.VMEM((NR, NT), BF16),
+            pltpu.VMEM((NT, NR), BF16),
             pltpu.VMEM((64, 128), F32),
             pltpu.VMEM((64, 128), F32),
             pltpu.VMEM((128, 128), F32),
@@ -320,12 +331,12 @@
             pltpu.VMEM((N_BLK, 1, 128), F32),
             pltpu.VMEM((N_BLK, 1, 128), F32),
             pltpu.VMEM((N_BAND * N_BLK, 1, 128), F32),
-            pltpu.VMEM((32, N_BAND * 64), F32),
+            pltpu.VMEM((64, N_BAND * 64), F32),
             pltpu.VMEM((R, N_BAND * 128, B), BF16),
             pltpu.VMEM((R, A_OWN, N_BAND * 64), F32),
             pltpu.VMEM((R, A_OWN, N_BAND * 64), F32),
             pltpu.VMEM((64, 128), F32),
-            pltpu.VMEM((4 * NR, 128), BF16),
+            pltpu.VMEM((NR, NR), BF16),
             *([dma] * 9),
         ],
         compiler_params=pltpu.CompilerParams(collective_id=0, has_side_effects=True, vmem_limit_bytes=67043328),

time: 30.1 us -> 29.7 us (0.987)
  Pallas kernels: 28.3 us -> 27.9 us
    pallas_call x1, Pallas kernels: 28.3 us -> 27.9 us  [per_device(): pl.pallas_call(kernel, out_shape=jax.ShapeDtypeStruct((2 * A_OWN * R, B),...]
where the time goes in v3:
time: 29.7 us; the launch traced here: 29.6 us
  Pallas kernels  27.9 us (94%)
  local copies, waits for them, and re-layouts  1.67 us (6%)
    pallas_call x1, Pallas kernels, per_device(): pl.pallas_call(kernel, out_shape=jax.ShapeDtypeStruct((2 * A_OWN * R, B),...  27.9 us
    unnamed x1, local copies, waits for them, and re-layouts  1.67 us

profile of v3, /device:TPU:1, one launch (start us, length us, event | category | flops | bytes accessed | tf_op | source)
XLA Modules:
  0.0 29.6 jit_solution(9725125843976533108)
XLA Ops:
  0.0 27.9 %shard_map.55 = f32[512,128]{1,0:T(8,128)} custom-call(s32[8]{0:T(128)} %counts_in.1, f32[2048,128]{1,0:T(8,128)} %bitcast.15, bf16[512,4096]{1,0:T(8,128)(2,1)} %bitcast.13, f32[64,128]{1,0:T(8,128)} %bitcast.16, f32[64,128]{1,0:T(8,128)} %bitcast.17), custom_call_target="tpu_custom_call" | custom-call | tf_op jit(solution)/shard_map/pallas_call | solution.py:317
  27.9 1.7 %copy.7 = f32[2,8,4096]{2,1,0:T(8,128)} copy(f32[2,8,4096]{2,1,0:T(8,128)} %bitcast.14) | data formatting | bytes 524288

commit v4 on v3

--- a/solution.py
+++ b/solution.py
@@ -339,8 +339,8 @@
             pltpu.VMEM((NR, NR), BF16),
             *([dma] * 9),
         ],
-        compiler_params=pltpu.CompilerParams(collective_id=0, has_side_effects=True, vmem_limit_bytes=67043328),
-    )(cycle_counts, sky, leg, signal_power.reshape(64, 128), noise_power.reshape(64, 128))
+        compiler_params=pltpu.CompilerParams(collective_id=0, has_side_effects=True, vmem_limit_bytes=32 << 20),
+    )(*[pltpu.with_memory_space_constraint(x, pltpu.HBM) for x in (cycle_counts, sky, leg, signal_power.reshape(64, 128), noise_power.reshape(64, 128))])
     return result.reshape(2, A_OWN, R, B).transpose(0, 2, 1, 3).reshape(2, R, A_OWN * B)
 
 

time: 29.7 us -> 28 us (0.943)
  local copies, waits for them, and re-layouts: 1.67 us -> 0.71 us
  Pallas kernels: 27.9 us -> 27.2 us
    unnamed x1, local copies, waits for them, and re-layouts: 1.67 us -> 0.71 us
    pallas_call x1, Pallas kernels: 27.9 us -> 27.2 us  [per_device(): pl.pallas_call(kernel, out_shape=jax.ShapeDtypeStruct((2 * A_OWN * R, B),...]
where the time goes in v4:
time: 28 us; the launch traced here: 27.9 us
  Pallas kernels  27.2 us (97%)
  local copies, waits for them, and re-layouts  0.71 us (3%)
    pallas_call x1, Pallas kernels, per_device(): pl.pallas_call(kernel, out_shape=jax.ShapeDtypeStruct((2 * A_OWN * R, B),...  27.2 us
    unnamed x1, local copies, waits for them, and re-layouts  0.71 us

profile of v4, /device:TPU:1, one launch (start us, length us, event | category | flops | bytes accessed | tf_op | source)
XLA Modules:
  0.0 27.9 jit_solution(14187394722926669812)
XLA Ops:
  0.0 27.2 %shard_map.55 = f32[512,128]{1,0:T(8,128)S(1)} custom-call(s32[8]{0:T(128)} %counts_in.1, f32[2048,128]{1,0:T(8,128)} %bitcast.15, bf16[512,4096]{1,0:T(8,128)(2,1)} %bitcast.14, f32[64,128]{1,0:T(8,128)} %bitcast.16, f32[64,128]{1,0:T(8,128)} %bitcast.17), custom_call_target="tpu_custom_call" | custom-call | tf_op jit(solution)/shard_map/pallas_call | solution.py:317
  27.2 0.7 %copy.7 = f32[2,8,4096]{2,1,0:T(8,128)} copy(f32[2,8,4096]{2,1,0:T(8,128)S(1)} %bitcast.13) | data formatting | bytes 524288

commit v5 on v4

--- a/solution.py
+++ b/solution.py
@@ -81,6 +81,10 @@
 ):
     blk = lax.axis_index("blk")
     band = lax.axis_index("band")
+    count_copy = pltpu.make_async_copy(counts_in, counts, count_sem)
+    count_copy.start()
+    sky_copy = pltpu.make_async_copy(sky, xs, sky_sem)
+    sky_copy.start()
     barrier = pltpu.get_barrier_semaphore()
 
     ys = [lax.rem(lax.div(blk, 16) + d, 4) * 16 for d in range(4)]
@@ -98,10 +102,6 @@
         pl.semaphore_signal(barrier, inc=1, device_id=(peer, band), device_id_type=MESH)
     for e in range(1, N_BAND):
         pl.semaphore_signal(barrier, inc=1, device_id=(blk, lax.rem(band + e, N_BAND)), device_id_type=MESH)
-    count_copy = pltpu.make_async_copy(counts_in, counts, count_sem)
-    count_copy.start()
-    sky_copy = pltpu.make_async_copy(sky, xs, sky_sem)
-    sky_copy.start()
     leg_copy = pltpu.make_async_copy(leg, legv, leg_sem)
     leg_copy.start()
     signal_copy = pltpu.make_async_copy(signal_in, signal, signal_sem)

time: 28 us -> 27.7 us (0.989)
  Pallas kernels: 27.2 us -> 26.9 us
where the time goes in v5:
time: 27.7 us; the launch traced here: 27.6 us
  Pallas kernels  26.9 us (97%)
  local copies, waits for them, and re-layouts  0.71 us (3%)
    pallas_call x1, Pallas kernels, per_device(): pl.pallas_call(kernel, out_shape=jax.ShapeDtypeStruct((2 * A_OWN * R, B),...  26.9 us
    unnamed x1, local copies, waits for them, and re-layouts  0.71 us

profile of v5, /device:TPU:1, one launch (start us, length us, event | category | flops | bytes accessed | tf_op | source)
XLA Modules:
  0.0 27.6 jit_solution(18269736550414143112)
XLA Ops:
  0.0 26.9 %shard_map.55 = f32[512,128]{1,0:T(8,128)S(1)} custom-call(s32[8]{0:T(128)} %counts_in.1, f32[2048,128]{1,0:T(8,128)} %bitcast.15, bf16[512,4096]{1,0:T(8,128)(2,1)} %bitcast.14, f32[64,128]{1,0:T(8,128)} %bitcast.16, f32[64,128]{1,0:T(8,128)} %bitcast.17), custom_call_target="tpu_custom_call" | custom-call | tf_op jit(solution)/shard_map/pallas_call | solution.py:317
  26.9 0.7 %copy.7 = f32[2,8,4096]{2,1,0:T(8,128)} copy(f32[2,8,4096]{2,1,0:T(8,128)S(1)} %bitcast.13) | data formatting | bytes 524288
